TPU v7x, 32 devices: a whole 2x2x4 slice. The times are simulated.
32 devices in a mesh: member: 2 (over core), shard: 16 (over z, y, x).
Axes of the slice: x: 2, y: 2, z: 4, core: 2. Of those that a mesh axis runs over, the one named last changes fastest.
Arguments:
- layer_input: bfloat16 [2, 180, 5120], P('member', None, 'shard'), may hold values from -6 to 6
- norm_gain: float32 [2, 5120], P('member'), may hold values from 0.5 to 2
- w_gate: bfloat16 [2, 5120, 1792], P('member', None, 'shard'), may hold values from -0.0559017 to 0.0559017
- w_up: bfloat16 [2, 5120, 1792], P('member', None, 'shard'), may hold values from -0.0559017 to 0.0559017
- hidden_cot: bfloat16 [2, 180, 1792], P('member', None, 'shard'), may hold values from -3 to 5
- output_cot: bfloat16 [2, 180, 5120], P('member', None, 'shard'), may hold values from -6 to 6
- embed: bfloat16 [2, 4096, 5120], P('member', 'shard'), may hold values from -0.078125 to 0.078125
- suffix_ids: int32 [180], replicated, may hold values from 0 to 4095
Outputs:
- delta: float32 [180, 4096], P(None, 'shard')
All inputs are finite; a program needn't handle non-finite values.
Results may differ from a plain program's by a relative error of at most 0.0047.
Values may be sent and summed in bfloat16 or wider, within the bound.
A program may use at most 64 MiB of HBM per device.

v0:
```python
import jax
import jax.numpy as jnp
from jax import lax
from jax.sharding import PartitionSpec as P


def on_device(layer_input, norm_gain, w_gate, w_up, hidden_cot, output_cot, embed, suffix_ids):
    input_local = layer_input[0]
    cot_local = output_cot[0]
    gain = norm_gain[0]
    gate_w = w_gate[0]
    up_w = w_up[0]
    table = embed[0]
    whole_input = lax.all_gather(input_local, "shard", axis=1, tiled=True)
    inputs = whole_input.astype(jnp.float32)
    width = inputs.shape[1]
    inv_rms = 1.0 / jnp.sqrt(jnp.mean(inputs * inputs, axis=1, keepdims=True) + 1e-05)
    normed = (inputs * inv_rms * gain[None, :]).astype(jnp.bfloat16)
    gate_pre = jnp.dot(normed, gate_w, preferred_element_type=jnp.float32)
    up_proj = jnp.dot(normed, up_w, preferred_element_type=jnp.float32)
    sigmoid_gate = jax.nn.sigmoid(gate_pre)
    hid_f = hidden_cot[0].astype(jnp.float32)
    gate_grad = (hid_f * up_proj * sigmoid_gate * (1.0 + gate_pre * (1.0 - sigmoid_gate))).astype(
        jnp.bfloat16
    )
    up_grad = (hid_f * gate_pre * sigmoid_gate).astype(jnp.bfloat16)
    contract = (((1,), (1,)), ((), ()))
    share_width = input_local.shape[1]
    part = lax.dot_general(gate_w, gate_grad, contract, preferred_element_type=jnp.float32)
    share_t = lax.psum_scatter(
        part + lax.dot_general(up_w, up_grad, contract, preferred_element_type=jnp.float32),
        "shard",
        scatter_dimension=0,
        tiled=True,
    )
    share = share_t.T
    offset = lax.axis_index("shard") * share_width
    gain_share = lax.dynamic_slice_in_dim(gain, offset, share_width, 0)
    input_share = input_local.astype(jnp.float32)
    scaled = share * gain_share[None, :]
    partial_proj = jnp.sum(input_share * scaled, axis=1)
    proj = lax.psum(partial_proj, "shard")[:, None] / width
    grad_share = cot_local.astype(jnp.float32) + inv_rms * scaled - input_share * inv_rms**3 * proj
    grad_share = grad_share.astype(jnp.bfloat16)
    scores = lax.dot_general(
        lax.all_gather(grad_share, "shard", axis=1, tiled=True),
        table,
        contract,
        preferred_element_type=jnp.float32,
    )
    vocab_local = table.shape[0]
    first_entry = lax.axis_index("shard") * vocab_local
    entries = first_entry + lax.broadcasted_iota(jnp.int32, (1, vocab_local), 1)
    own_mask = (suffix_ids[:, None] == entries).astype(jnp.float32)
    own_local = jnp.sum(scores * own_mask, axis=1)
    current = lax.psum(own_local, "shard")
    delta = lax.psum(scores - current[:, None], "member")
    return delta


def solution(mesh):
    placed = (
        P("member", None, "shard"),
        P("member", None),
        P("member", None, "shard"),
        P("member", None, "shard"),
        P("member", None, "shard"),
        P("member", None, "shard"),
        P("member", "shard", None),
        P(),
    )
    return jax.shard_map(
        on_device, mesh=mesh, in_specs=placed, out_specs=P(None, "shard"), check_vma=False
    )
```

profile of v0, /device:TPU:0, one launch (start us, length us, event | category | flops | bytes accessed | tf_op | source)
XLA Modules:
  0.0 417.3 jit_solution(5285484548928964807)
XLA Ops:
  6.5 0.0 copy-start
  6.5 0.0 all-gather.5.cloned.1.call-start
  6.5 2.0 copy.12
  8.5 0.0 all-gather.5.cloned.1.call-update
  8.6 0.0 reduce-scatter.4.cloned.1.call-start
  8.6 88.6 %all-gather.5.cloned.1.call-done = bf16[1,180,5120]{1,0,2:T(2,128)(2,1)} async-done(((bf16[1,180,320]{1,0,2:T(2,128)(2,1)}), bf16[1,180,5120]{1,0,2:T(2,128)(2,1)}) %all-gather.5.cloned.1.call-update) | async-done | bytes 1843216 | tf_op jit(solution)/shard_map/all_gather | solution.py:14
  97.2 0.0 copy-start.5
  97.2 11.0 %copy.13 = bf16[1,180,5120]{2,1,0:T(8,128)(2,1)} copy(bf16[1,180,5120]{1,0,2:T(2,128)(2,1)} %all-gather.5.cloned.1.call-done) | data formatting | bytes 3686400 | tf_op jit(solution)/shard_map/all_gather | solution.py:14
  108.2 0.0 copy-start.1
  108.2 2.1 fusion.1
  110.3 0.0 copy-done.5
  110.3 0.0 copy-done.1
  110.3 0.0 copy-start.3
  110.3 2.1 fusion.8
  112.4 0.0 copy-done.3
  112.5 6.2 %fusion.6 = f32[180,5120]{1,0:T(8,128)} fusion(bf16[1,5120,112]{1,2,0:T(8,128)(2,1)} %param.10, bf16[1,5120,112]{1,2,0:T(8,128)(2,1)} %param.11, bf16[1,180,5120]{2,1,0:T(8,128)(2,1)} %copy.13, f32[5120]{0:T(1024)S(1)} %bitcast.68, f32[180]{0:T(256)S(1)} %get-tuple-element.6, f32[180,112]{1,0:T(8,128)S(1)} %fusion.8, bf16[1,180,112]{2,1,0:T(8,128)(2,1)S(1)} %copy-done.3), kind=kOutput, calls=%fused_computation.9 | convolution fusion | flops 416784960 | bytes 7965520 | tf_op jit(solution)/shard_map/dot_general | solution.py:29
  118.7 4.9 %fusion = f32[5120,180]{0,1:T(8,128)} fusion(f32[180,5120]{1,0:T(8,128)} %fusion.6, bf16[1,5120,112]{1,2,0:T(8,128)(2,1)} %param.11, f32[180,112]{1,0:T(8,128)S(1)} %fusion.8, bf16[1,180,112]{2,1,0:T(8,128)(2,1)S(1)} %copy-done.3), kind=kOutput, calls=%fused_computation.1 | convolution fusion | flops 207501120 | bytes 8640640 | tf_op jit(solution)/shard_map/dot_general | solution.py:31
  123.6 5.6 %copy.15 = f32[5120,180]{1,0:T(8,128)} copy(f32[5120,180]{0,1:T(8,128)} %fusion) | data formatting | bytes 7372800
  129.2 0.0 copy-start.2
  129.2 0.0 copy-start.4
  129.2 0.0 reduce-scatter.4.cloned.1.call-update
  129.3 0.0 all-gather.7.cloned.1.call-start
  129.3 0.1 dynamic-slice_reduce_fusion
  129.4 114.3 %reduce-scatter.4.cloned.1.call-done = f32[320,180]{1,0:T(8,128)} async-done(((f32[5120,180]{1,0:T(8,128)}), f32[320,180]{1,0:T(8,128)}) %reduce-scatter.4.cloned.1.call-update) | async-done | bytes 230416
  243.7 1.1 copy.16
  244.9 0.0 copy-done.2
  244.9 0.1 fusion.33
  245.0 41.3 %psum.21 = f32[180]{0:T(256)S(1)} all-reduce(f32[180]{0:T(256)S(1)} %fusion.33), channel_id=1, replica_groups=mesh['member'=2,'shard'=16] {'shard'}, use_global_device_ids=true, to_apply=%region_3.0 | all-reduce | flops 180 | bytes 1440 | tf_op jit(solution)/shard_map/psum | solution.py:42
  286.3 0.0 copy-done.4
  286.3 0.8 fusion.34
  287.1 0.0 all-gather.7.cloned.1.call-update
  287.1 0.0 all-reduce.2.cloned.1.call-start
  287.2 57.4 %all-gather.7.cloned.1.call-done = bf16[16,320,180]{1,2,0:T(8,128)(2,1)} async-done(((bf16[1,320,180]{1,2,0:T(8,128)(2,1)}), bf16[16,320,180]{1,2,0:T(8,128)(2,1)}) %all-gather.7.cloned.1.call-update) | async-done | bytes 1843216 | tf_op jit(solution)/shard_map/all_gather | solution.py:46
  344.6 3.3 copy.14
  347.9 0.0 copy-start.6
  347.9 4.5 %reshape.35 = bf16[5120,180]{0,1:T(8,128)(2,1)} reshape(bf16[16,320,180]{1,0,2:T(8,128)(2,1)} %copy.14) | data formatting | bytes 3686400
  352.5 0.0 copy-done
  352.5 0.0 copy-done.6
  352.5 2.6 select_reduce_fusion
  355.1 39.2 %psum.22 = f32[180]{0:T(256)S(1)} all-reduce(f32[180]{0:T(256)S(1)} %get-tuple-element.7), channel_id=1, replica_groups=mesh['member'=2,'shard'=16] {'shard'}, use_global_device_ids=true, to_apply=%region_5.0 | all-reduce | flops 180 | bytes 1440 | tf_op jit(solution)/shard_map/psum | solution.py:56
  394.3 0.8 broadcast_subtract_fusion
  395.1 0.0 all-reduce.2.cloned.1.call-update
  395.1 14.1 %all-reduce.2.cloned.1.call-done = f32[180,256]{1,0:T(8,128)} async-done(((f32[180,256]{1,0:T(8,128)}), f32[180,256]{1,0:T(8,128)}) %all-reduce.2.cloned.1.call-update) | async-done | bytes 184336 | tf_op jit(solution)/shard_map/psum | solution.py:57
  409.2 1.6 copy.18
  (3 shorter events, 0.0 us)
Async XLA Ops:
  6.5 345.9 %copy-start = (bf16[1,256,5120]{2,1,0:T(8,128)(2,1)S(1)}, bf16[1,256,5120]{2,1,0:T(8,128)(2,1)}, u32[]{:S(2)}) copy-start(bf16[1,256,5120]{2,1,0:T(8,128)(2,1)} %param.14) | copy-start | bytes 7864324
  6.5 90.6 %all-gather.5.cloned.1.call-start = ((), (), s32[]{:S(2)}) async-start(), calls=%async_computation.2 | async-start | bytes 5570560 | tf_op jit(solution)/shard_map/all_gather | solution.py:14
  8.6 235.2 %reduce-scatter.4.cloned.1.call-start = ((), (), s32[]{:S(2)}) async-start(), calls=%async_computation.4 | async-start | bytes 5570560
  97.2 13.1 %copy-start.5 = (f32[1,5120]{1,0:T(1,128)S(1)}, f32[1,5120]{1,0:T(1,128)}, u32[]{:S(2)}) copy-start(f32[1,5120]{1,0:T(1,128)} %param.9) | copy-start | bytes 61444
  108.2 2.1 copy-start.1
  110.3 2.1 copy-start.3
  129.2 115.6 %copy-start.2 = (bf16[1,180,320]{2,1,0:T(8,128)(2,1)S(1)}, bf16[1,180,320]{2,1,0:T(8,128)(2,1)}, u32[]{:S(2)}) copy-start(bf16[1,180,320]{2,1,0:T(8,128)(2,1)} %param.8) | copy-start | bytes 345604
  129.2 157.0 %copy-start.4 = (bf16[1,180,320]{2,1,0:T(8,128)(2,1)S(1)}, bf16[1,180,320]{2,1,0:T(8,128)(2,1)}, u32[]{:S(2)}) copy-start(bf16[1,180,320]{2,1,0:T(8,128)(2,1)} %param.13) | copy-start | bytes 345604
  129.3 215.4 %all-gather.7.cloned.1.call-start = ((), (), s32[]{:S(2)}) async-start(), calls=%async_computation.3 | async-start | bytes 2402304 | tf_op jit(solution)/shard_map/all_gather | solution.py:46
  287.1 122.0 %all-reduce.2.cloned.1.call-start = ((), (), s32[]{:S(2)}) async-start(), calls=%async_computation.1 | async-start | bytes 376832 | tf_op jit(solution)/shard_map/psum | solution.py:57
  347.9 4.5 %copy-start.6 = (s32[180]{0:T(256)S(1)}, s32[180]{0:T(256)}, u32[]{:S(2)}) copy-start(s32[180]{0:T(256)} %param.15) | copy-start | bytes 2164
Sparse Core Ops, SparseCore 0:
  10.1 87.0 all-gather.4
  129.4 114.3 reduce-scatter.3
  287.3 57.3 all-gather.6
  395.2 13.8 all-reduce.1
where the time goes:
time: 418 us; the launch traced here: 417 us
  waiting for transfers between devices  274 us (66%)
  blocking collectives  80.5 us (19%)
  local copies, waits for them, and re-layouts  29.3 us (7%)
  matrix products  15.9 us (4%)
  between operations  13.2 us (3%)
    unnamed x5, waiting for transfers between devices  114 us
    all_gather x1, waiting for transfers between devices, on_device(): whole_input = lax.all_gather(input_local, 'shard', axis=1, tiled=True)  88.6 us
    all_gather x1, waiting for transfers between devices, on_device(): lax.all_gather(grad_share, 'shard', axis=1, tiled=True)  57.4 us
    psum x1, blocking collectives, on_device(): proj = lax.psum(partial_proj, 'shard')[:, None] / width  41.3 us
    psum x1, blocking collectives, on_device(): current = lax.psum(own_local, 'shard')  39.2 us
    unnamed x19, local copies, waits for them, and re-layouts  14.9 us
    psum x1, waiting for transfers between devices, on_device(): delta = lax.psum(scores - current[:, None], 'member')  14.1 us
    all_gather x1, local copies, waits for them, and re-layouts, on_device(): whole_input = lax.all_gather(input_local, 'shard', axis=1, tiled=True)  11 us
  transfers between devices with their start and end apart: 4, of which 4 were waited for; matrix products, arithmetic and copies ran while one was open for 0% of the time, Pallas kernels for 0%

commit v1 on v0

--- a/solution.py
+++ b/solution.py
@@ -53,7 +53,8 @@
     entries = first_entry + lax.broadcasted_iota(jnp.int32, (1, vocab_local), 1)
     own_mask = (suffix_ids[:, None] == entries).astype(jnp.float32)
     own_local = jnp.sum(scores * own_mask, axis=1)
-    current = lax.psum(own_local, "shard")
+    shards = lax.all_gather(own_local, "shard")
+    current = jnp.sum(shards, axis=0)
     delta = lax.psum(scores - current[:, None], "member")
     return delta
 

time: 418 us -> 453 us (1.084)
  blocking collectives: 80.5 us -> 115 us
    unnamed x0 -> x1, blocking collectives: none -> 74.2 us
    psum x1 -> x0, blocking collectives: 39.2 us -> none  [on_device(): current = lax.psum(own_local, 'shard')]
    unnamed x19 -> x24, local copies, waits for them, and re-layouts: 14.9 us -> 15.9 us
where the time goes in v1:
time: 453 us
  waiting for transfers between devices  273 us (60%)
  blocking collectives  115 us (25%)
  local copies, waits for them, and re-layouts  30.3 us (7%)
  matrix products  15.9 us (4%)
  between operations  13.9 us (3%)
    unnamed x5, waiting for transfers between devices  114 us
    all_gather x1, waiting for transfers between devices, on_device(): whole_input = lax.all_gather(input_local, 'shard', axis=1, tiled=True)  88.6 us
    unnamed x1, blocking collectives  74.2 us
    all_gather x1, waiting for transfers between devices, on_device(): lax.all_gather(grad_share, 'shard', axis=1, tiled=True)  56 us
    psum x1, blocking collectives, on_device(): proj = lax.psum(partial_proj, 'shard')[:, None] / width  41.3 us
    unnamed x24, local copies, waits for them, and re-layouts  15.9 us
    psum x1, waiting for transfers between devices, on_device(): delta = lax.psum(scores - current[:, None], 'member')  14 us
    all_gather x1, local copies, waits for them, and re-layouts, on_device(): whole_input = lax.all_gather(input_local, 'shard', axis=1, tiled=True)  11 us
  transfers between devices with their start and end apart: 4, of which 4 were waited for; matrix products, arithmetic and copies ran while one was open for 0% of the time, Pallas kernels for 0%

profile of v1, /device:TPU:0, one launch (start us, length us, event | category | flops | bytes accessed | tf_op | source)
XLA Modules:
  0.0 452.7 jit_solution(8464161942415167688)
XLA Ops:
  6.5 0.0 copy-start
  6.5 0.0 all-gather.6.cloned.1.call-start
  6.5 2.0 copy.15
  8.5 0.0 all-gather.6.cloned.1.call-update
  8.6 0.0 reduce-scatter.4.cloned.1.call-start
  8.6 88.6 %all-gather.6.cloned.1.call-done = bf16[1,180,5120]{1,0,2:T(2,128)(2,1)} async-done(((bf16[1,180,320]{1,0,2:T(2,128)(2,1)}), bf16[1,180,5120]{1,0,2:T(2,128)(2,1)}) %all-gather.6.cloned.1.call-update) | async-done | bytes 1843216 | tf_op jit(solution)/shard_map/all_gather | solution.py:14
  97.2 0.0 copy-start.5
  97.2 11.0 %copy.16 = bf16[1,180,5120]{2,1,0:T(8,128)(2,1)} copy(bf16[1,180,5120]{1,0,2:T(2,128)(2,1)} %all-gather.6.cloned.1.call-done) | data formatting | bytes 3686400 | tf_op jit(solution)/shard_map/all_gather | solution.py:14
  108.2 0.0 copy-start.1
  108.2 2.1 fusion.1
  110.3 0.0 copy-done.5
  110.3 0.0 copy-done.1
  110.3 0.0 copy-start.3
  110.3 2.1 fusion.8
  112.4 0.0 copy-done.3
  112.5 6.2 %fusion.6 = f32[180,5120]{1,0:T(8,128)} fusion(bf16[1,5120,112]{1,2,0:T(8,128)(2,1)} %param.10, bf16[1,5120,112]{1,2,0:T(8,128)(2,1)} %param.11, bf16[1,180,5120]{2,1,0:T(8,128)(2,1)} %copy.16, f32[5120]{0:T(1024)S(1)} %bitcast.69, f32[180]{0:T(256)S(1)} %get-tuple-element.6, f32[180,112]{1,0:T(8,128)S(1)} %fusion.8, bf16[1,180,112]{2,1,0:T(8,128)(2,1)S(1)} %copy-done.3), kind=kOutput, calls=%fused_computation.9 | convolution fusion | flops 416784960 | bytes 7965520 | tf_op jit(solution)/shard_map/dot_general | solution.py:29
  118.7 4.9 %fusion = f32[5120,180]{0,1:T(8,128)} fusion(f32[180,5120]{1,0:T(8,128)} %fusion.6, bf16[1,5120,112]{1,2,0:T(8,128)(2,1)} %param.11, f32[180,112]{1,0:T(8,128)S(1)} %fusion.8, bf16[1,180,112]{2,1,0:T(8,128)(2,1)S(1)} %copy-done.3), kind=kOutput, calls=%fused_computation.1 | convolution fusion | flops 207501120 | bytes 8640640 | tf_op jit(solution)/shard_map/dot_general | solution.py:31
  123.6 5.6 %copy.18 = f32[5120,180]{1,0:T(8,128)} copy(f32[5120,180]{0,1:T(8,128)} %fusion) | data formatting | bytes 7372800
  129.2 0.0 copy-start.2
  129.2 0.0 copy-start.4
  129.2 0.0 reduce-scatter.4.cloned.1.call-update
  129.3 0.0 copy-start.7
  129.3 0.0 all-gather.8.cloned.1.call-start
  129.3 0.1 dynamic-slice_reduce_fusion
  129.4 114.3 %reduce-scatter.4.cloned.1.call-done = f32[320,180]{1,0:T(8,128)} async-done(((f32[5120,180]{1,0:T(8,128)}), f32[320,180]{1,0:T(8,128)}) %reduce-scatter.4.cloned.1.call-update) | async-done | bytes 230416
  243.7 1.1 copy.19
  244.9 0.0 copy-done.2
  244.9 0.1 fusion.33
  245.0 41.3 %psum.14 = f32[180]{0:T(256)S(1)} all-reduce(f32[180]{0:T(256)S(1)} %fusion.33), channel_id=1, replica_groups=mesh['member'=2,'shard'=16] {'shard'}, use_global_device_ids=true, to_apply=%region_3.0 | all-reduce | flops 180 | bytes 1440 | tf_op jit(solution)/shard_map/psum | solution.py:42
  286.3 0.0 copy-done.4
  286.3 0.8 fusion.34
  287.1 0.0 all-gather.8.cloned.1.call-update
  287.1 0.0 all-reduce.3.cloned.1.call-start
  287.2 0.0 copy-done.7
  287.2 0.7 dynamic-slice.1
  288.6 56.0 %all-gather.8.cloned.1.call-done = bf16[16,320,180]{1,2,0:T(8,128)(2,1)} async-done(((bf16[1,320,180]{1,2,0:T(8,128)(2,1)}), bf16[16,320,180]{1,2,0:T(8,128)(2,1)}) %all-gather.8.cloned.1.call-update) | async-done | bytes 1843216 | tf_op jit(solution)/shard_map/all_gather | solution.py:46
  344.6 3.3 copy.17
  347.9 0.0 copy-start.6
  347.9 4.5 %reshape.39 = bf16[5120,180]{0,1:T(8,128)(2,1)} reshape(bf16[16,320,180]{1,0,2:T(8,128)(2,1)} %copy.17) | data formatting | bytes 3686400
  352.4 0.0 copy-done
  352.4 0.0 copy-done.6
  352.4 2.6 select_reduce_fusion
  355.1 0.3 dynamic-update-slice
  355.4 74.2 %all-reduce = f32[2880]{0:T(1024)S(1)} all-reduce(f32[2880]{0:T(1024)S(1)} %dynamic-update-slice), channel_id=3, replica_groups=mesh['member'=2,'shard'=16] {'shard'}, use_global_device_ids=true, to_apply=%add | all-reduce | flops 2880 | bytes 23040
  429.6 0.1 reshape.32
  429.7 0.8 broadcast_subtract_fusion
  430.5 0.0 all-reduce.3.cloned.1.call-update
  430.5 14.0 %all-reduce.3.cloned.1.call-done = f32[180,256]{1,0:T(8,128)} async-done(((f32[180,256]{1,0:T(8,128)}), f32[180,256]{1,0:T(8,128)}) %all-reduce.3.cloned.1.call-update) | async-done | bytes 184336 | tf_op jit(solution)/shard_map/psum | solution.py:58
  444.6 1.6 copy.22
  (5 shorter events, 0.0 us)
Async XLA Ops:
  6.5 345.9 %copy-start = (bf16[1,256,5120]{2,1,0:T(8,128)(2,1)S(1)}, bf16[1,256,5120]{2,1,0:T(8,128)(2,1)}, u32[]{:S(2)}) copy-start(bf16[1,256,5120]{2,1,0:T(8,128)(2,1)} %param.14) | copy-start | bytes 7864324
  6.5 90.6 %all-gather.6.cloned.1.call-start = ((), (), s32[]{:S(2)}) async-start(), calls=%async_computation.2 | async-start | bytes 5570560 | tf_op jit(solution)/shard_map/all_gather | solution.py:14
  8.6 235.2 %reduce-scatter.4.cloned.1.call-start = ((), (), s32[]{:S(2)}) async-start(), calls=%async_computation.4 | async-start | bytes 5570560
  97.2 13.1 %copy-start.5 = (f32[1,5120]{1,0:T(1,128)S(1)}, f32[1,5120]{1,0:T(1,128)}, u32[]{:S(2)}) copy-start(f32[1,5120]{1,0:T(1,128)} %param.9) | copy-start | bytes 61444
  108.2 2.1 copy-start.1
  110.3 2.1 copy-start.3
  129.2 115.6 %copy-start.2 = (bf16[1,180,320]{2,1,0:T(8,128)(2,1)S(1)}, bf16[1,180,320]{2,1,0:T(8,128)(2,1)}, u32[]{:S(2)}) copy-start(bf16[1,180,320]{2,1,0:T(8,128)(2,1)} %param.8) | copy-start | bytes 345604
  129.2 157.0 %copy-start.4 = (bf16[1,180,320]{2,1,0:T(8,128)(2,1)S(1)}, bf16[1,180,320]{2,1,0:T(8,128)(2,1)}, u32[]{:S(2)}) copy-start(bf16[1,180,320]{2,1,0:T(8,128)(2,1)} %param.13) | copy-start | bytes 345604
  129.3 157.9 %copy-start.7 = (u32[32]{0:T(128)S(1)}, u32[32]{0:T(128)}, u32[]{:S(2)}) copy-start(u32[32]{0:T(128)} %constant.34) | copy-start | bytes 388
  129.3 215.3 %all-gather.8.cloned.1.call-start = ((), (), s32[]{:S(2)}) async-start(), calls=%async_computation.3 | async-start | bytes 2402304 | tf_op jit(solution)/shard_map/all_gather | solution.py:46
  287.1 157.4 %all-reduce.3.cloned.1.call-start = ((), (), s32[]{:S(2)}) async-start(), calls=%async_computation.1 | async-start | bytes 376832 | tf_op jit(solution)/shard_map/psum | solution.py:58
  347.9 4.5 %copy-start.6 = (s32[180]{0:T(256)S(1)}, s32[180]{0:T(256)}, u32[]{:S(2)}) copy-start(s32[180]{0:T(256)} %param.15) | copy-start | bytes 2164
Sparse Core Ops, SparseCore 0:
  10.1 87.0 all-gather.5
  129.4 114.3 reduce-scatter.3
  287.3 57.3 all-gather.7
  430.6 13.8 all-reduce.2
